TPU v7x, 256 devices: a whole 4x4x8 slice. The times are simulated.
256 devices in a mesh: row: 16 (over z, core), col: 16 (over x, y).
Axes of the slice: x: 4, y: 4, z: 8, core: 2. Of those that a mesh axis runs over, the one named last changes fastest.
Arguments:
- rhs: float32 [16, 64, 128], P('col'), may hold values from -6 to 6
- diag_inv: float32 [16, 128, 128], P('col'), as said below
- panel: bfloat16 [16, 16, 128, 128], P('row', 'col'), may hold values from -0.09375 to 0.09375
- offdiag: bfloat16 [1024, 16, 128, 128], P('row', 'col'), may hold values from -0.015625 to 0.015625
- known: bfloat16 [512, 64, 128], P(('row', 'col')), may hold values from -6 to 6
- row_index: int32 [1024], P('row'), may hold values from 0 to 31
Outputs:
- solution: bfloat16 [16, 64, 128], P('col')
Inputs may be any that keep to these rules, and one draw needn't show every extreme that they name: Each block of diag_inv is lower triangular (the inverse of a lower triangular diagonal block).
All inputs are finite; a program needn't handle non-finite values.
Results may differ from a plain program's by a relative error of at most 0.015.
Values may be sent and summed in bfloat16 or wider, within the bound.
A program may use at most 64 MiB of HBM per device.

v0:
```python
import jax
import jax.numpy as jnp
from jax import lax
from jax.sharding import PartitionSpec as P

NB = 16


def spread(array, axis, root):
    mine = lax.axis_index(axis) == root
    return lax.psum(jnp.where(mine, array, jnp.zeros_like(array)), axis)


def finish_block(total, inverse, turn_block, root, solved):
    local = jnp.dot(
        total, inverse, precision=lax.Precision.HIGHEST, preferred_element_type=jnp.float32
    ).astype(jnp.bfloat16)
    block = spread(local, "col", root)
    solved = lax.dynamic_update_index_in_dim(solved, block, turn_block, 0)
    return (block, solved)


def body(rhs, diag_inv, panel, offdiag, known, row_index):
    rows_count = lax.axis_size("row")
    cols_count = lax.axis_size("col")
    row_id = lax.axis_index("row")
    col_id = lax.axis_index("col")
    col_slots = NB // cols_count
    known_row = lax.all_gather(known, "col", axis=0, tiled=True)
    picked = jnp.take(known_row, row_index, axis=0)
    off_part = jnp.einsum("pqi,pbia->bqa", picked, offdiag, preferred_element_type=jnp.float32)
    off_sum = lax.psum(off_part, "row")
    update = rhs - off_sum
    col_global = jnp.arange(col_slots) * cols_count + col_id
    accum = jnp.zeros(update.shape, jnp.float32)
    solved = jnp.zeros((NB,) + update.shape[1:], jnp.bfloat16)

    def step_reduced(turn, carry):
        sums, result = carry
        block_id = NB - 1 - turn
        slot = block_id // cols_count
        partial_value = lax.dynamic_index_in_dim(sums, slot, 0, keepdims=False)
        summed = lax.psum(partial_value.astype(jnp.bfloat16), "row").astype(jnp.float32)
        total = lax.dynamic_index_in_dim(update, slot, 0, keepdims=False) - summed
        inverse = lax.dynamic_index_in_dim(diag_inv, slot, 0, keepdims=False)
        block, result = finish_block(total, inverse, block_id, block_id % cols_count, result)
        tiles = lax.dynamic_index_in_dim(panel, block_id // rows_count, 0, keepdims=False)
        contrib = jnp.einsum("qi,bia->bqa", block, tiles, preferred_element_type=jnp.float32)
        keep = (col_global < block_id) & (block_id % rows_count == row_id)
        return (sums + jnp.where(keep[:, None, None], contrib, 0.0), result)

    accum, solved = lax.fori_loop(0, NB, step_reduced, (accum, solved))
    return jnp.take(solved, col_global, axis=0)


def solution(mesh):
    placed = (
        P("col", None, None),
        P("col", None, None),
        P("row", "col", None, None),
        P("row", "col", None, None),
        P(("row", "col"), None, None),
        P("row"),
    )
    return jax.shard_map(
        body, mesh=mesh, in_specs=placed, out_specs=P("col", None, None), check_vma=False
    )
```

profile of v0, /device:TPU:0, one launch (start us, length us, event | category | flops | bytes accessed | tf_op | source)
XLA Modules:
  0.0 1928.7 jit_solution(12652828160161664547)
XLA Ops:
  0.0 22.6 %all_gather.3 = bf16[32,64,128]{2,1,0:T(8,128)(2,1)S(1)} all-gather(bf16[2,64,128]{2,1,0:T(8,128)(2,1)} %param.12), channel_id=1, replica_groups=mesh['row'=16,'col'=16] {'col'}, dimensions={0}, use_global_device_ids=true | all-gather | bytes 557056 | tf_op jit(solution)/shard_map/all_gather | solution.py:29
  22.7 0.7 compare_select_fusion
  23.3 1.7 gather_fusion
  25.0 1.8 fusion.9
  26.9 48.6 %psum.35 = f32[1,64,128]{2,1,0:T(8,128)S(1)} all-reduce(f32[1,64,128]{2,1,0:T(8,128)S(1)} %fusion.9), channel_id=1, replica_groups=mesh['row'=16,'col'=16] {'row'}, use_global_device_ids=true, to_apply=%region_0.1 | all-reduce | flops 8192 | bytes 65536 | tf_op jit(solution)/shard_map/psum | solution.py:32
  75.6 1852.5 %while.19 = (s32[]{:T(128)}, f32[1,64,128]{2,1,0:T(8,128)S(1)}, bf16[16,64,128]{2,1,0:T(8,128)(2,1)S(1)}, s32[1]{0:T(128)}, s32[]{:T(128)}, /*index=5*/f32[1,64,...) while((s32[]{:T(128)}, f32[1,64,128]{2,1,0:T(8,128)S(1)}, ...), condition=%wide.region_4.5_spmd.clone, body=%wide.region_1.0_spmd.clone.sunk | while | flops 14762007 | bytes 393562 | solution.py:52
  75.6 45.7 %psum.40 = bf16[64,128]{1,0:T(8,128)(2,1)S(1)} all-reduce(bf16[64,128]{1,0:T(8,128)(2,1)S(1)} %fusion.26), channel_id=1, replica_groups=mesh['row'=16,'col'=16] {'row'}, use_global_device_ids=true, to_apply=%region_2.2 | all-reduce | flops 8192 | bytes 32768 | tf_op jit(solution)/shard_map/while/body/eval_jaxpr/psum | solution.py:43
  121.4 0.2 fusion.27
  121.5 72.1 %psum.41 = bf16[64,128]{1,0:T(8,128)(2,1)S(1)} all-reduce(bf16[64,128]{1,0:T(8,128)(2,1)S(1)} %fusion.27), channel_id=1, replica_groups=mesh['row'=16,'col'=16] {'col'}, use_global_device_ids=true, to_apply=%region_3.3 | all-reduce | flops 8192 | bytes 32768 | tf_op jit(solution)/shard_map/while/body/eval_jaxpr/psum | solution.py:11
  193.8 45.7 %psum.40 = bf16[64,128]{1,0:T(8,128)(2,1)S(1)} all-reduce(bf16[64,128]{1,0:T(8,128)(2,1)S(1)} %fusion.26), channel_id=1, replica_groups=mesh['row'=16,'col'=16] {'row'}, use_global_device_ids=true, to_apply=%region_2.2 | all-reduce | flops 8192 | bytes 32768 | tf_op jit(solution)/shard_map/while/body/eval_jaxpr/psum | solution.py:43
  239.7 69.6 %psum.41 = bf16[64,128]{1,0:T(8,128)(2,1)S(1)} all-reduce(bf16[64,128]{1,0:T(8,128)(2,1)S(1)} %fusion.27), channel_id=1, replica_groups=mesh['row'=16,'col'=16] {'col'}, use_global_device_ids=true, to_apply=%region_3.3 | all-reduce | flops 8192 | bytes 32768 | tf_op jit(solution)/shard_map/while/body/eval_jaxpr/psum | solution.py:11
  309.4 45.7 %psum.40 = bf16[64,128]{1,0:T(8,128)(2,1)S(1)} all-reduce(bf16[64,128]{1,0:T(8,128)(2,1)S(1)} %fusion.26), channel_id=1, replica_groups=mesh['row'=16,'col'=16] {'row'}, use_global_device_ids=true, to_apply=%region_2.2 | all-reduce | flops 8192 | bytes 32768 | tf_op jit(solution)/shard_map/while/body/eval_jaxpr/psum | solution.py:43
  355.1 0.2 fusion.27
  355.3 69.6 %psum.41 = bf16[64,128]{1,0:T(8,128)(2,1)S(1)} all-reduce(bf16[64,128]{1,0:T(8,128)(2,1)S(1)} %fusion.27), channel_id=1, replica_groups=mesh['row'=16,'col'=16] {'col'}, use_global_device_ids=true, to_apply=%region_3.3 | all-reduce | flops 8192 | bytes 32768 | tf_op jit(solution)/shard_map/while/body/eval_jaxpr/psum | solution.py:11
  425.0 45.7 %psum.40 = bf16[64,128]{1,0:T(8,128)(2,1)S(1)} all-reduce(bf16[64,128]{1,0:T(8,128)(2,1)S(1)} %fusion.26), channel_id=1, replica_groups=mesh['row'=16,'col'=16] {'row'}, use_global_device_ids=true, to_apply=%region_2.2 | all-reduce | flops 8192 | bytes 32768 | tf_op jit(solution)/shard_map/while/body/eval_jaxpr/psum | solution.py:43
  470.7 0.2 fusion.27
  470.9 69.6 %psum.41 = bf16[64,128]{1,0:T(8,128)(2,1)S(1)} all-reduce(bf16[64,128]{1,0:T(8,128)(2,1)S(1)} %fusion.27), channel_id=1, replica_groups=mesh['row'=16,'col'=16] {'col'}, use_global_device_ids=true, to_apply=%region_3.3 | all-reduce | flops 8192 | bytes 32768 | tf_op jit(solution)/shard_map/while/body/eval_jaxpr/psum | solution.py:11
  540.6 45.7 %psum.40 = bf16[64,128]{1,0:T(8,128)(2,1)S(1)} all-reduce(bf16[64,128]{1,0:T(8,128)(2,1)S(1)} %fusion.26), channel_id=1, replica_groups=mesh['row'=16,'col'=16] {'row'}, use_global_device_ids=true, to_apply=%region_2.2 | all-reduce | flops 8192 | bytes 32768 | tf_op jit(solution)/shard_map/while/body/eval_jaxpr/psum | solution.py:43
  586.6 69.6 %psum.41 = bf16[64,128]{1,0:T(8,128)(2,1)S(1)} all-reduce(bf16[64,128]{1,0:T(8,128)(2,1)S(1)} %fusion.27), channel_id=1, replica_groups=mesh['row'=16,'col'=16] {'col'}, use_global_device_ids=true, to_apply=%region_3.3 | all-reduce | flops 8192 | bytes 32768 | tf_op jit(solution)/shard_map/while/body/eval_jaxpr/psum | solution.py:11
  656.3 45.7 %psum.40 = bf16[64,128]{1,0:T(8,128)(2,1)S(1)} all-reduce(bf16[64,128]{1,0:T(8,128)(2,1)S(1)} %fusion.26), channel_id=1, replica_groups=mesh['row'=16,'col'=16] {'row'}, use_global_device_ids=true, to_apply=%region_2.2 | all-reduce | flops 8192 | bytes 32768 | tf_op jit(solution)/shard_map/while/body/eval_jaxpr/psum | solution.py:43
  702.0 0.2 fusion.27
  702.2 69.6 %psum.41 = bf16[64,128]{1,0:T(8,128)(2,1)S(1)} all-reduce(bf16[64,128]{1,0:T(8,128)(2,1)S(1)} %fusion.27), channel_id=1, replica_groups=mesh['row'=16,'col'=16] {'col'}, use_global_device_ids=true, to_apply=%region_3.3 | all-reduce | flops 8192 | bytes 32768 | tf_op jit(solution)/shard_map/while/body/eval_jaxpr/psum | solution.py:11
  771.9 45.7 %psum.40 = bf16[64,128]{1,0:T(8,128)(2,1)S(1)} all-reduce(bf16[64,128]{1,0:T(8,128)(2,1)S(1)} %fusion.26), channel_id=1, replica_groups=mesh['row'=16,'col'=16] {'row'}, use_global_device_ids=true, to_apply=%region_2.2 | all-reduce | flops 8192 | bytes 32768 | tf_op jit(solution)/shard_map/while/body/eval_jaxpr/psum | solution.py:43
  817.6 0.2 fusion.27
  817.8 69.6 %psum.41 = bf16[64,128]{1,0:T(8,128)(2,1)S(1)} all-reduce(bf16[64,128]{1,0:T(8,128)(2,1)S(1)} %fusion.27), channel_id=1, replica_groups=mesh['row'=16,'col'=16] {'col'}, use_global_device_ids=true, to_apply=%region_3.3 | all-reduce | flops 8192 | bytes 32768 | tf_op jit(solution)/shard_map/while/body/eval_jaxpr/psum | solution.py:11
  887.5 45.7 %psum.40 = bf16[64,128]{1,0:T(8,128)(2,1)S(1)} all-reduce(bf16[64,128]{1,0:T(8,128)(2,1)S(1)} %fusion.26), channel_id=1, replica_groups=mesh['row'=16,'col'=16] {'row'}, use_global_device_ids=true, to_apply=%region_2.2 | all-reduce | flops 8192 | bytes 32768 | tf_op jit(solution)/shard_map/while/body/eval_jaxpr/psum | solution.py:43
  933.2 0.2 fusion.27
  933.4 69.6 %psum.41 = bf16[64,128]{1,0:T(8,128)(2,1)S(1)} all-reduce(bf16[64,128]{1,0:T(8,128)(2,1)S(1)} %fusion.27), channel_id=1, replica_groups=mesh['row'=16,'col'=16] {'col'}, use_global_device_ids=true, to_apply=%region_3.3 | all-reduce | flops 8192 | bytes 32768 | tf_op jit(solution)/shard_map/while/body/eval_jaxpr/psum | solution.py:11
  1003.1 45.7 %psum.40 = bf16[64,128]{1,0:T(8,128)(2,1)S(1)} all-reduce(bf16[64,128]{1,0:T(8,128)(2,1)S(1)} %fusion.26), channel_id=1, replica_groups=mesh['row'=16,'col'=16] {'row'}, use_global_device_ids=true, to_apply=%region_2.2 | all-reduce | flops 8192 | bytes 32768 | tf_op jit(solution)/shard_map/while/body/eval_jaxpr/psum | solution.py:43
  1048.8 0.2 fusion.27
  1049.0 69.6 %psum.41 = bf16[64,128]{1,0:T(8,128)(2,1)S(1)} all-reduce(bf16[64,128]{1,0:T(8,128)(2,1)S(1)} %fusion.27), channel_id=1, replica_groups=mesh['row'=16,'col'=16] {'col'}, use_global_device_ids=true, to_apply=%region_3.3 | all-reduce | flops 8192 | bytes 32768 | tf_op jit(solution)/shard_map/while/body/eval_jaxpr/psum | solution.py:11
  1118.7 45.7 %psum.40 = bf16[64,128]{1,0:T(8,128)(2,1)S(1)} all-reduce(bf16[64,128]{1,0:T(8,128)(2,1)S(1)} %fusion.26), channel_id=1, replica_groups=mesh['row'=16,'col'=16] {'row'}, use_global_device_ids=true, to_apply=%region_2.2 | all-reduce | flops 8192 | bytes 32768 | tf_op jit(solution)/shard_map/while/body/eval_jaxpr/psum | solution.py:43
  1164.5 0.2 fusion.27
  1164.7 69.6 %psum.41 = bf16[64,128]{1,0:T(8,128)(2,1)S(1)} all-reduce(bf16[64,128]{1,0:T(8,128)(2,1)S(1)} %fusion.27), channel_id=1, replica_groups=mesh['row'=16,'col'=16] {'col'}, use_global_device_ids=true, to_apply=%region_3.3 | all-reduce | flops 8192 | bytes 32768 | tf_op jit(solution)/shard_map/while/body/eval_jaxpr/psum | solution.py:11
  1234.4 45.7 %psum.40 = bf16[64,128]{1,0:T(8,128)(2,1)S(1)} all-reduce(bf16[64,128]{1,0:T(8,128)(2,1)S(1)} %fusion.26), channel_id=1, replica_groups=mesh['row'=16,'col'=16] {'row'}, use_global_device_ids=true, to_apply=%region_2.2 | all-reduce | flops 8192 | bytes 32768 | tf_op jit(solution)/shard_map/while/body/eval_jaxpr/psum | solution.py:43
  1280.3 69.6 %psum.41 = bf16[64,128]{1,0:T(8,128)(2,1)S(1)} all-reduce(bf16[64,128]{1,0:T(8,128)(2,1)S(1)} %fusion.27), channel_id=1, replica_groups=mesh['row'=16,'col'=16] {'col'}, use_global_device_ids=true, to_apply=%region_3.3 | all-reduce | flops 8192 | bytes 32768 | tf_op jit(solution)/shard_map/while/body/eval_jaxpr/psum | solution.py:11
  1350.0 45.7 %psum.40 = bf16[64,128]{1,0:T(8,128)(2,1)S(1)} all-reduce(bf16[64,128]{1,0:T(8,128)(2,1)S(1)} %fusion.26), channel_id=1, replica_groups=mesh['row'=16,'col'=16] {'row'}, use_global_device_ids=true, to_apply=%region_2.2 | all-reduce | flops 8192 | bytes 32768 | tf_op jit(solution)/shard_map/while/body/eval_jaxpr/psum | solution.py:43
  1395.7 0.2 fusion.27
  1395.9 69.6 %psum.41 = bf16[64,128]{1,0:T(8,128)(2,1)S(1)} all-reduce(bf16[64,128]{1,0:T(8,128)(2,1)S(1)} %fusion.27), channel_id=1, replica_groups=mesh['row'=16,'col'=16] {'col'}, use_global_device_ids=true, to_apply=%region_3.3 | all-reduce | flops 8192 | bytes 32768 | tf_op jit(solution)/shard_map/while/body/eval_jaxpr/psum | solution.py:11
  1465.6 45.7 %psum.40 = bf16[64,128]{1,0:T(8,128)(2,1)S(1)} all-reduce(bf16[64,128]{1,0:T(8,128)(2,1)S(1)} %fusion.26), channel_id=1, replica_groups=mesh['row'=16,'col'=16] {'row'}, use_global_device_ids=true, to_apply=%region_2.2 | all-reduce | flops 8192 | bytes 32768 | tf_op jit(solution)/shard_map/while/body/eval_jaxpr/psum | solution.py:43
  1511.5 69.6 %psum.41 = bf16[64,128]{1,0:T(8,128)(2,1)S(1)} all-reduce(bf16[64,128]{1,0:T(8,128)(2,1)S(1)} %fusion.27), channel_id=1, replica_groups=mesh['row'=16,'col'=16] {'col'}, use_global_device_ids=true, to_apply=%region_3.3 | all-reduce | flops 8192 | bytes 32768 | tf_op jit(solution)/shard_map/while/body/eval_jaxpr/psum | solution.py:11
  1581.2 45.7 %psum.40 = bf16[64,128]{1,0:T(8,128)(2,1)S(1)} all-reduce(bf16[64,128]{1,0:T(8,128)(2,1)S(1)} %fusion.26), channel_id=1, replica_groups=mesh['row'=16,'col'=16] {'row'}, use_global_device_ids=true, to_apply=%region_2.2 | all-reduce | flops 8192 | bytes 32768 | tf_op jit(solution)/shard_map/while/body/eval_jaxpr/psum | solution.py:43
  1627.1 69.6 %psum.41 = bf16[64,128]{1,0:T(8,128)(2,1)S(1)} all-reduce(bf16[64,128]{1,0:T(8,128)(2,1)S(1)} %fusion.27), channel_id=1, replica_groups=mesh['row'=16,'col'=16] {'col'}, use_global_device_ids=true, to_apply=%region_3.3 | all-reduce | flops 8192 | bytes 32768 | tf_op jit(solution)/shard_map/while/body/eval_jaxpr/psum | solution.py:11
  1696.8 45.7 %psum.40 = bf16[64,128]{1,0:T(8,128)(2,1)S(1)} all-reduce(bf16[64,128]{1,0:T(8,128)(2,1)S(1)} %fusion.26), channel_id=1, replica_groups=mesh['row'=16,'col'=16] {'row'}, use_global_device_ids=true, to_apply=%region_2.2 | all-reduce | flops 8192 | bytes 32768 | tf_op jit(solution)/shard_map/while/body/eval_jaxpr/psum | solution.py:43
  1742.7 69.6 %psum.41 = bf16[64,128]{1,0:T(8,128)(2,1)S(1)} all-reduce(bf16[64,128]{1,0:T(8,128)(2,1)S(1)} %fusion.27), channel_id=1, replica_groups=mesh['row'=16,'col'=16] {'col'}, use_global_device_ids=true, to_apply=%region_3.3 | all-reduce | flops 8192 | bytes 32768 | tf_op jit(solution)/shard_map/while/body/eval_jaxpr/psum | solution.py:11
  1812.5 45.7 %psum.40 = bf16[64,128]{1,0:T(8,128)(2,1)S(1)} all-reduce(bf16[64,128]{1,0:T(8,128)(2,1)S(1)} %fusion.26), channel_id=1, replica_groups=mesh['row'=16,'col'=16] {'row'}, use_global_device_ids=true, to_apply=%region_2.2 | all-reduce | flops 8192 | bytes 32768 | tf_op jit(solution)/shard_map/while/body/eval_jaxpr/psum | solution.py:43
  1858.4 69.6 %psum.41 = bf16[64,128]{1,0:T(8,128)(2,1)S(1)} all-reduce(bf16[64,128]{1,0:T(8,128)(2,1)S(1)} %fusion.27), channel_id=1, replica_groups=mesh['row'=16,'col'=16] {'col'}, use_global_device_ids=true, to_apply=%region_3.3 | all-reduce | flops 8192 | bytes 32768 | tf_op jit(solution)/shard_map/while/body/eval_jaxpr/psum | solution.py:11
  1928.1 0.6 dynamic-slice_select_fusion
  (70 shorter events, 3.7 us)
Async XLA Ops:
  0.0 25.0 %copy-start = (bf16[64,1,128,128]{3,2,1,0:T(8,128)(2,1)S(1)}, bf16[64,1,128,128]{3,2,1,0:T(8,128)(2,1)}, u32[]{:S(2)}) copy-start(bf16[64,1,128,128]{3,2,1,0:T(8,128)(2,1)} %param.11) | copy-start | bytes 6291460
  0.0 25.0 %copy-start.4 = (s32[64]{0:T(128)S(1)}, s32[64]{0:T(128)}, u32[]{:S(2)}) copy-start(s32[64]{0:T(128)} %param.13) | copy-start | bytes 772
  25.0 50.5 %copy-start.3 = (f32[1,64,128]{2,1,0:T(8,128)S(1)}, f32[1,64,128]{2,1,0:T(8,128)}, u32[]{:S(2)}) copy-start(f32[1,64,128]{2,1,0:T(8,128)} %param.8) | copy-start | bytes 98308
  25.0 50.6 %copy-start.1 = (f32[1,128,128]{2,1,0:T(8,128)S(1)}, f32[1,128,128]{2,1,0:T(8,128)}, u32[]{:S(2)}) copy-start(f32[1,128,128]{2,1,0:T(8,128)} %param.9) | copy-start | bytes 196612
  25.0 50.6 %copy-start.2 = (bf16[1,1,128,128]{3,2,1,0:T(8,128)(2,1)S(1)}, bf16[1,1,128,128]{3,2,1,0:T(8,128)(2,1)}, u32[]{:S(2)}) copy-start(bf16[1,1,128,128]{3,2,1,0:T(8,128)(2,1)} %param.10) | copy-start | bytes 98308
where the time goes:
time: 1930 us
  blocking collectives  1920 us (99%)
    psum x16, blocking collectives, spread(): return lax.psum(jnp.where(mine, array, jnp.zeros_like(array)), axis)  1120 us
    psum x16, blocking collectives, step_reduced(): lax.psum(partial_value.astype(jnp.bfloat16), 'row').astype(jnp.float32)  732 us
    psum x1, blocking collectives, body(): off_sum = lax.psum(off_part, 'row')  48.6 us

commit v1 on v0

--- a/solution.py
+++ b/solution.py
@@ -29,7 +29,9 @@
     known_row = lax.all_gather(known, "col", axis=0, tiled=True)
     picked = jnp.take(known_row, row_index, axis=0)
     off_part = jnp.einsum("pqi,pbia->bqa", picked, offdiag, preferred_element_type=jnp.float32)
-    off_sum = lax.psum(off_part, "row")
+    off_sum = off_part
+    for hop in (1, 2, 4, 8):
+        off_sum = off_sum + lax.ppermute(off_sum, "row", [(dev, dev ^ hop) for dev in range(16)])
     update = rhs - off_sum
     col_global = jnp.arange(col_slots) * cols_count + col_id
     accum = jnp.zeros(update.shape, jnp.float32)

time: 1930 us -> 1900 us (0.984)
  blocking collectives: 1920 us -> 1870 us
    psum x1 -> x0, blocking collectives: 48.6 us -> none  [body(): off_sum = lax.psum(off_part, 'row')]
  transfers between devices with their start and end apart: 0 -> 4, of which waited for: 0 -> 4; matrix products, arithmetic and copies ran while one was open for 0% -> 0% of each run, Pallas kernels for 0% -> 0%
where the time goes in v1:
time: 1900 us
  blocking collectives  1870 us (98%)
    psum x16, blocking collectives, spread(): return lax.psum(jnp.where(mine, array, jnp.zeros_like(array)), axis)  1120 us
    psum x16, blocking collectives, step_reduced(): lax.psum(partial_value.astype(jnp.bfloat16), 'row').astype(jnp.float32)  733 us
  transfers between devices with their start and end apart: 4, of which 4 were waited for; matrix products, arithmetic and copies ran while one was open for 0% of the time, Pallas kernels for 0%

profile of v1, /device:TPU:0, one launch (start us, length us, event | category | flops | bytes accessed | tf_op | source)
XLA Modules:
  0.0 1901.5 jit_solution(4550065972621105938)
XLA Ops:
  0.0 0.8 compare_select_fusion
  0.8 0.7 compare_and_fusion
  1.5 22.5 %all_gather.3 = bf16[32,64,128]{2,1,0:T(8,128)(2,1)S(1)} all-gather(bf16[2,64,128]{2,1,0:T(8,128)(2,1)} %param.12), channel_id=1, replica_groups=mesh['row'=16,'col'=16] {'col'}, dimensions={0}, use_global_device_ids=true | all-gather | bytes 557056 | tf_op jit(solution)/shard_map/all_gather | solution.py:29
  24.0 1.6 gather_fusion
  25.7 1.8 fusion.9
  27.6 1.2 collective-permute-done
  28.8 1.9 collective-permute-start.1
  30.7 2.0 collective-permute-done.1
  32.7 3.3 collective-permute-start.2
  36.0 1.9 collective-permute-done.2
  37.9 6.8 collective-permute-start.3
  44.7 1.9 collective-permute-done.3
  46.7 1854.1 %while.19 = (s32[]{:T(128)}, f32[1,64,128]{2,1,0:T(8,128)S(1)}, bf16[16,64,128]{2,1,0:T(8,128)(2,1)S(1)}, s32[1]{0:T(128)}, s32[]{:T(128)}, /*index=5*/f32[1,64,...) while((s32[]{:T(128)}, f32[1,64,128]{2,1,0:T(8,128)S(1)}, ...), condition=%wide.region_3.4_spmd.clone, body=%wide.region_0.3_spmd.clone.sunk | while | flops 14762007 | bytes 393562 | solution.py:54
  46.8 47.4 %psum.32 = bf16[64,128]{1,0:T(8,128)(2,1)S(1)} all-reduce(bf16[64,128]{1,0:T(8,128)(2,1)S(1)} %fusion.26), channel_id=1, replica_groups=mesh['row'=16,'col'=16] {'row'}, use_global_device_ids=true, to_apply=%region_1.1 | all-reduce | flops 8192 | bytes 32768 | tf_op jit(solution)/shard_map/while/body/eval_jaxpr/psum | solution.py:45
  94.1 0.2 fusion.27
  94.3 72.1 %psum.33 = bf16[64,128]{1,0:T(8,128)(2,1)S(1)} all-reduce(bf16[64,128]{1,0:T(8,128)(2,1)S(1)} %fusion.27), channel_id=1, replica_groups=mesh['row'=16,'col'=16] {'col'}, use_global_device_ids=true, to_apply=%region_2.2 | all-reduce | flops 8192 | bytes 32768 | tf_op jit(solution)/shard_map/while/body/eval_jaxpr/psum | solution.py:11
  166.6 45.7 %psum.32 = bf16[64,128]{1,0:T(8,128)(2,1)S(1)} all-reduce(bf16[64,128]{1,0:T(8,128)(2,1)S(1)} %fusion.26), channel_id=1, replica_groups=mesh['row'=16,'col'=16] {'row'}, use_global_device_ids=true, to_apply=%region_1.1 | all-reduce | flops 8192 | bytes 32768 | tf_op jit(solution)/shard_map/while/body/eval_jaxpr/psum | solution.py:45
  212.3 0.2 fusion.27
  212.5 69.6 %psum.33 = bf16[64,128]{1,0:T(8,128)(2,1)S(1)} all-reduce(bf16[64,128]{1,0:T(8,128)(2,1)S(1)} %fusion.27), channel_id=1, replica_groups=mesh['row'=16,'col'=16] {'col'}, use_global_device_ids=true, to_apply=%region_2.2 | all-reduce | flops 8192 | bytes 32768 | tf_op jit(solution)/shard_map/while/body/eval_jaxpr/psum | solution.py:11
  282.2 45.7 %psum.32 = bf16[64,128]{1,0:T(8,128)(2,1)S(1)} all-reduce(bf16[64,128]{1,0:T(8,128)(2,1)S(1)} %fusion.26), channel_id=1, replica_groups=mesh['row'=16,'col'=16] {'row'}, use_global_device_ids=true, to_apply=%region_1.1 | all-reduce | flops 8192 | bytes 32768 | tf_op jit(solution)/shard_map/while/body/eval_jaxpr/psum | solution.py:45
  328.1 69.6 %psum.33 = bf16[64,128]{1,0:T(8,128)(2,1)S(1)} all-reduce(bf16[64,128]{1,0:T(8,128)(2,1)S(1)} %fusion.27), channel_id=1, replica_groups=mesh['row'=16,'col'=16] {'col'}, use_global_device_ids=true, to_apply=%region_2.2 | all-reduce | flops 8192 | bytes 32768 | tf_op jit(solution)/shard_map/while/body/eval_jaxpr/psum | solution.py:11
  397.8 45.7 %psum.32 = bf16[64,128]{1,0:T(8,128)(2,1)S(1)} all-reduce(bf16[64,128]{1,0:T(8,128)(2,1)S(1)} %fusion.26), channel_id=1, replica_groups=mesh['row'=16,'col'=16] {'row'}, use_global_device_ids=true, to_apply=%region_1.1 | all-reduce | flops 8192 | bytes 32768 | tf_op jit(solution)/shard_map/while/body/eval_jaxpr/psum | solution.py:45
  443.7 69.6 %psum.33 = bf16[64,128]{1,0:T(8,128)(2,1)S(1)} all-reduce(bf16[64,128]{1,0:T(8,128)(2,1)S(1)} %fusion.27), channel_id=1, replica_groups=mesh['row'=16,'col'=16] {'col'}, use_global_device_ids=true, to_apply=%region_2.2 | all-reduce | flops 8192 | bytes 32768 | tf_op jit(solution)/shard_map/while/body/eval_jaxpr/psum | solution.py:11
  513.4 45.7 %psum.32 = bf16[64,128]{1,0:T(8,128)(2,1)S(1)} all-reduce(bf16[64,128]{1,0:T(8,128)(2,1)S(1)} %fusion.26), channel_id=1, replica_groups=mesh['row'=16,'col'=16] {'row'}, use_global_device_ids=true, to_apply=%region_1.1 | all-reduce | flops 8192 | bytes 32768 | tf_op jit(solution)/shard_map/while/body/eval_jaxpr/psum | solution.py:45
  559.3 69.6 %psum.33 = bf16[64,128]{1,0:T(8,128)(2,1)S(1)} all-reduce(bf16[64,128]{1,0:T(8,128)(2,1)S(1)} %fusion.27), channel_id=1, replica_groups=mesh['row'=16,'col'=16] {'col'}, use_global_device_ids=true, to_apply=%region_2.2 | all-reduce | flops 8192 | bytes 32768 | tf_op jit(solution)/shard_map/while/body/eval_jaxpr/psum | solution.py:11
  629.1 45.7 %psum.32 = bf16[64,128]{1,0:T(8,128)(2,1)S(1)} all-reduce(bf16[64,128]{1,0:T(8,128)(2,1)S(1)} %fusion.26), channel_id=1, replica_groups=mesh['row'=16,'col'=16] {'row'}, use_global_device_ids=true, to_apply=%region_1.1 | all-reduce | flops 8192 | bytes 32768 | tf_op jit(solution)/shard_map/while/body/eval_jaxpr/psum | solution.py:45
  675.0 69.6 %psum.33 = bf16[64,128]{1,0:T(8,128)(2,1)S(1)} all-reduce(bf16[64,128]{1,0:T(8,128)(2,1)S(1)} %fusion.27), channel_id=1, replica_groups=mesh['row'=16,'col'=16] {'col'}, use_global_device_ids=true, to_apply=%region_2.2 | all-reduce | flops 8192 | bytes 32768 | tf_op jit(solution)/shard_map/while/body/eval_jaxpr/psum | solution.py:11
  744.7 45.7 %psum.32 = bf16[64,128]{1,0:T(8,128)(2,1)S(1)} all-reduce(bf16[64,128]{1,0:T(8,128)(2,1)S(1)} %fusion.26), channel_id=1, replica_groups=mesh['row'=16,'col'=16] {'row'}, use_global_device_ids=true, to_apply=%region_1.1 | all-reduce | flops 8192 | bytes 32768 | tf_op jit(solution)/shard_map/while/body/eval_jaxpr/psum | solution.py:45
  790.6 69.6 %psum.33 = bf16[64,128]{1,0:T(8,128)(2,1)S(1)} all-reduce(bf16[64,128]{1,0:T(8,128)(2,1)S(1)} %fusion.27), channel_id=1, replica_groups=mesh['row'=16,'col'=16] {'col'}, use_global_device_ids=true, to_apply=%region_2.2 | all-reduce | flops 8192 | bytes 32768 | tf_op jit(solution)/shard_map/while/body/eval_jaxpr/psum | solution.py:11
  860.3 45.7 %psum.32 = bf16[64,128]{1,0:T(8,128)(2,1)S(1)} all-reduce(bf16[64,128]{1,0:T(8,128)(2,1)S(1)} %fusion.26), channel_id=1, replica_groups=mesh['row'=16,'col'=16] {'row'}, use_global_device_ids=true, to_apply=%region_1.1 | all-reduce | flops 8192 | bytes 32768 | tf_op jit(solution)/shard_map/while/body/eval_jaxpr/psum | solution.py:45
  906.2 69.6 %psum.33 = bf16[64,128]{1,0:T(8,128)(2,1)S(1)} all-reduce(bf16[64,128]{1,0:T(8,128)(2,1)S(1)} %fusion.27), channel_id=1, replica_groups=mesh['row'=16,'col'=16] {'col'}, use_global_device_ids=true, to_apply=%region_2.2 | all-reduce | flops 8192 | bytes 32768 | tf_op jit(solution)/shard_map/while/body/eval_jaxpr/psum | solution.py:11
  975.9 45.7 %psum.32 = bf16[64,128]{1,0:T(8,128)(2,1)S(1)} all-reduce(bf16[64,128]{1,0:T(8,128)(2,1)S(1)} %fusion.26), channel_id=1, replica_groups=mesh['row'=16,'col'=16] {'row'}, use_global_device_ids=true, to_apply=%region_1.1 | all-reduce | flops 8192 | bytes 32768 | tf_op jit(solution)/shard_map/while/body/eval_jaxpr/psum | solution.py:45
  1021.8 69.6 %psum.33 = bf16[64,128]{1,0:T(8,128)(2,1)S(1)} all-reduce(bf16[64,128]{1,0:T(8,128)(2,1)S(1)} %fusion.27), channel_id=1, replica_groups=mesh['row'=16,'col'=16] {'col'}, use_global_device_ids=true, to_apply=%region_2.2 | all-reduce | flops 8192 | bytes 32768 | tf_op jit(solution)/shard_map/while/body/eval_jaxpr/psum | solution.py:11
  1091.5 45.7 %psum.32 = bf16[64,128]{1,0:T(8,128)(2,1)S(1)} all-reduce(bf16[64,128]{1,0:T(8,128)(2,1)S(1)} %fusion.26), channel_id=1, replica_groups=mesh['row'=16,'col'=16] {'row'}, use_global_device_ids=true, to_apply=%region_1.1 | all-reduce | flops 8192 | bytes 32768 | tf_op jit(solution)/shard_map/while/body/eval_jaxpr/psum | solution.py:45
  1137.4 69.6 %psum.33 = bf16[64,128]{1,0:T(8,128)(2,1)S(1)} all-reduce(bf16[64,128]{1,0:T(8,128)(2,1)S(1)} %fusion.27), channel_id=1, replica_groups=mesh['row'=16,'col'=16] {'col'}, use_global_device_ids=true, to_apply=%region_2.2 | all-reduce | flops 8192 | bytes 32768 | tf_op jit(solution)/shard_map/while/body/eval_jaxpr/psum | solution.py:11
  1207.1 45.7 %psum.32 = bf16[64,128]{1,0:T(8,128)(2,1)S(1)} all-reduce(bf16[64,128]{1,0:T(8,128)(2,1)S(1)} %fusion.26), channel_id=1, replica_groups=mesh['row'=16,'col'=16] {'row'}, use_global_device_ids=true, to_apply=%region_1.1 | all-reduce | flops 8192 | bytes 32768 | tf_op jit(solution)/shard_map/while/body/eval_jaxpr/psum | solution.py:45
  1253.1 69.6 %psum.33 = bf16[64,128]{1,0:T(8,128)(2,1)S(1)} all-reduce(bf16[64,128]{1,0:T(8,128)(2,1)S(1)} %fusion.27), channel_id=1, replica_groups=mesh['row'=16,'col'=16] {'col'}, use_global_device_ids=true, to_apply=%region_2.2 | all-reduce | flops 8192 | bytes 32768 | tf_op jit(solution)/shard_map/while/body/eval_jaxpr/psum | solution.py:11
  1322.8 45.7 %psum.32 = bf16[64,128]{1,0:T(8,128)(2,1)S(1)} all-reduce(bf16[64,128]{1,0:T(8,128)(2,1)S(1)} %fusion.26), channel_id=1, replica_groups=mesh['row'=16,'col'=16] {'row'}, use_global_device_ids=true, to_apply=%region_1.1 | all-reduce | flops 8192 | bytes 32768 | tf_op jit(solution)/shard_map/while/body/eval_jaxpr/psum | solution.py:45
  1368.7 69.6 %psum.33 = bf16[64,128]{1,0:T(8,128)(2,1)S(1)} all-reduce(bf16[64,128]{1,0:T(8,128)(2,1)S(1)} %fusion.27), channel_id=1, replica_groups=mesh['row'=16,'col'=16] {'col'}, use_global_device_ids=true, to_apply=%region_2.2 | all-reduce | flops 8192 | bytes 32768 | tf_op jit(solution)/shard_map/while/body/eval_jaxpr/psum | solution.py:11
  1438.4 45.7 %psum.32 = bf16[64,128]{1,0:T(8,128)(2,1)S(1)} all-reduce(bf16[64,128]{1,0:T(8,128)(2,1)S(1)} %fusion.26), channel_id=1, replica_groups=mesh['row'=16,'col'=16] {'row'}, use_global_device_ids=true, to_apply=%region_1.1 | all-reduce | flops 8192 | bytes 32768 | tf_op jit(solution)/shard_map/while/body/eval_jaxpr/psum | solution.py:45
  1484.3 69.6 %psum.33 = bf16[64,128]{1,0:T(8,128)(2,1)S(1)} all-reduce(bf16[64,128]{1,0:T(8,128)(2,1)S(1)} %fusion.27), channel_id=1, replica_groups=mesh['row'=16,'col'=16] {'col'}, use_global_device_ids=true, to_apply=%region_2.2 | all-reduce | flops 8192 | bytes 32768 | tf_op jit(solution)/shard_map/while/body/eval_jaxpr/psum | solution.py:11
  1554.0 45.7 %psum.32 = bf16[64,128]{1,0:T(8,128)(2,1)S(1)} all-reduce(bf16[64,128]{1,0:T(8,128)(2,1)S(1)} %fusion.26), channel_id=1, replica_groups=mesh['row'=16,'col'=16] {'row'}, use_global_device_ids=true, to_apply=%region_1.1 | all-reduce | flops 8192 | bytes 32768 | tf_op jit(solution)/shard_map/while/body/eval_jaxpr/psum | solution.py:45
  1599.9 69.6 %psum.33 = bf16[64,128]{1,0:T(8,128)(2,1)S(1)} all-reduce(bf16[64,128]{1,0:T(8,128)(2,1)S(1)} %fusion.27), channel_id=1, replica_groups=mesh['row'=16,'col'=16] {'col'}, use_global_device_ids=true, to_apply=%region_2.2 | all-reduce | flops 8192 | bytes 32768 | tf_op jit(solution)/shard_map/while/body/eval_jaxpr/psum | solution.py:11
  1669.6 45.7 %psum.32 = bf16[64,128]{1,0:T(8,128)(2,1)S(1)} all-reduce(bf16[64,128]{1,0:T(8,128)(2,1)S(1)} %fusion.26), channel_id=1, replica_groups=mesh['row'=16,'col'=16] {'row'}, use_global_device_ids=true, to_apply=%region_1.1 | all-reduce | flops 8192 | bytes 32768 | tf_op jit(solution)/shard_map/while/body/eval_jaxpr/psum | solution.py:45
  1715.5 69.6 %psum.33 = bf16[64,128]{1,0:T(8,128)(2,1)S(1)} all-reduce(bf16[64,128]{1,0:T(8,128)(2,1)S(1)} %fusion.27), channel_id=1, replica_groups=mesh['row'=16,'col'=16] {'col'}, use_global_device_ids=true, to_apply=%region_2.2 | all-reduce | flops 8192 | bytes 32768 | tf_op jit(solution)/shard_map/while/body/eval_jaxpr/psum | solution.py:11
  1785.2 45.7 %psum.32 = bf16[64,128]{1,0:T(8,128)(2,1)S(1)} all-reduce(bf16[64,128]{1,0:T(8,128)(2,1)S(1)} %fusion.26), channel_id=1, replica_groups=mesh['row'=16,'col'=16] {'row'}, use_global_device_ids=true, to_apply=%region_1.1 | all-reduce | flops 8192 | bytes 32768 | tf_op jit(solution)/shard_map/while/body/eval_jaxpr/psum | solution.py:45
  1831.2 69.6 %psum.33 = bf16[64,128]{1,0:T(8,128)(2,1)S(1)} all-reduce(bf16[64,128]{1,0:T(8,128)(2,1)S(1)} %fusion.27), channel_id=1, replica_groups=mesh['row'=16,'col'=16] {'col'}, use_global_device_ids=true, to_apply=%region_2.2 | all-reduce | flops 8192 | bytes 32768 | tf_op jit(solution)/shard_map/while/body/eval_jaxpr/psum | solution.py:11
  1900.8 0.6 dynamic-slice_select_fusion
  (78 shorter events, 5.1 us)
Async XLA Ops:
  0.0 25.6 %copy-start = (bf16[64,1,128,128]{3,2,1,0:T(8,128)(2,1)S(1)}, bf16[64,1,128,128]{3,2,1,0:T(8,128)(2,1)}, u32[]{:S(2)}) copy-start(bf16[64,1,128,128]{3,2,1,0:T(8,128)(2,1)} %param.11) | copy-start | bytes 6291460
  25.6 21.0 %copy-start.3 = (f32[1,64,128]{2,1,0:T(8,128)S(1)}, f32[1,64,128]{2,1,0:T(8,128)}, u32[]{:S(2)}) copy-start(f32[1,64,128]{2,1,0:T(8,128)} %param.8) | copy-start | bytes 98308
  25.7 21.0 %copy-start.1 = (f32[1,128,128]{2,1,0:T(8,128)S(1)}, f32[1,128,128]{2,1,0:T(8,128)}, u32[]{:S(2)}) copy-start(f32[1,128,128]{2,1,0:T(8,128)} %param.9) | copy-start | bytes 196612
  25.7 21.1 %copy-start.2 = (bf16[1,1,128,128]{3,2,1,0:T(8,128)(2,1)S(1)}, bf16[1,1,128,128]{3,2,1,0:T(8,128)(2,1)}, u32[]{:S(2)}) copy-start(bf16[1,1,128,128]{3,2,1,0:T(8,128)(2,1)} %param.10) | copy-start | bytes 98308
  27.5 1.3 collective-permute-start
  28.8 3.9 collective-permute-start.1
  32.7 5.2 collective-permute-start.2
  37.9 8.7 collective-permute-start.3
